TPU v7x, 256 devices: a whole 4x4x8 slice. The times are simulated.
256 devices in a mesh: freq: 8 (over x, core), mode: 32 (over y, z).
Axes of the slice: x: 4, y: 4, z: 8, core: 2. Of those that a mesh axis runs over, the one named last changes fastest.
Arguments:
- mode_shapes: bfloat16 [6144, 12288], P(None, 'mode'), may hold values from -0.109375 to 0.109375
- modal_freq: float32 [12288], P('mode'), may hold values from 0.5 to 4
- damping: float32 [12288], P('mode'), may hold values from 0.05 to 0.2
- excitation: float32 [32], P('freq'), parts along dimension 0, may hold values from 0.5 to 4
- modal_load: float32 [12288, 32, 2, 64], P('mode', 'freq'), parts along dimension 1, may hold values from -6 to 6
- attach: int32 [32, 96], replicated, may hold values from 0 to 6143
- row_count: int32 [32], P('mode'), may hold values from 48 to 384, as said below
- otm: bfloat16 [32, 384, 96], P('mode'), may hold values from -0.625 to 0.625
Outputs:
- csd: bfloat16 [32, 32, 2, 384, 384], P('mode', 'freq'), parts along dimension 1
- joint_csd: bfloat16 [32, 32, 2, 128, 384], P('mode', 'freq'), parts along dimension 1
There are 8 independent parts, one for each index of `freq`. A program takes and returns all parts, laid end to end along the dimension named above; an argument that names none is the same for every part. Nothing has to cross between parts.
Inputs may be any that keep to these rules, and one draw needn't show every extreme that they name: `row_count`: at least one component has exactly 384 rows in every draw.
All inputs are finite; a program needn't handle non-finite values.
Results may differ from a plain program's by a relative error of at most 0.008.
Values may be sent and summed in bfloat16 or wider, within the bound.
A program may use at most 128 MiB of HBM per device.

v0:
```python
import jax
import jax.numpy as jnp
from jax import lax
from jax.sharding import PartitionSpec as P

CROSS = 128


def shifted(value, axis, steps):
    count = lax.axis_size(axis)
    initial, last = (max(0, -steps), min(count, count - steps))
    return lax.ppermute(value, axis, [(source, source + steps) for source in range(initial, last)])


def per_device(mode_shapes, modal_freq, damping, excitation, modal_load, attach, row_count, otm):
    comp_here = otm.shape[0]
    rows_max = otm.shape[1]
    att_len = otm.shape[2]
    lines = excitation.shape[0]
    width = modal_load.shape[3]
    columns = lines * 2 * width
    omega_sq = modal_freq * modal_freq
    real_part = omega_sq[:, None] - (excitation * excitation)[None, :]
    imag_part = 2.0 * damping[:, None] * modal_freq[:, None] * excitation[None, :]
    denom = real_part * real_part + imag_part * imag_part
    frf_re = (omega_sq[:, None] * real_part / denom)[:, :, None]
    frf_im = (-omega_sq[:, None] * imag_part / denom)[:, :, None]
    load_re = modal_load[:, :, 0, :]
    load_im = modal_load[:, :, 1, :]
    resp_re = frf_re * load_re - frf_im * load_im
    resp_im = frf_re * load_im + frf_im * load_re
    modal_resp = jnp.stack([resp_re, resp_im], axis=2).astype(jnp.bfloat16)
    modal_resp = modal_resp.reshape(modal_resp.shape[0], columns)
    flat_attach = attach.reshape(-1)
    own_start = lax.axis_index("mode") * (comp_here * att_len)
    band = lax.psum_scatter(
        jnp.dot(mode_shapes, modal_resp, preferred_element_type=jnp.float32),
        "mode",
        scatter_dimension=0,
        tiled=True,
    ).astype(jnp.bfloat16)
    whole = lax.all_gather(band, "mode", axis=0, tiled=True)
    index_rows = lax.dynamic_slice_in_dim(flat_attach, own_start, comp_here * att_len)
    picked = jnp.take(whole, index_rows, axis=0)
    picked = picked.reshape(comp_here, att_len, columns)
    row_mask = jnp.arange(rows_max, dtype=jnp.int32)[None, :] < row_count[:, None]
    masked_otm = jnp.where(row_mask[:, :, None], otm, jnp.zeros_like(otm))
    factor = jnp.einsum(
        "cra,caj->crj", masked_otm, picked, preferred_element_type=jnp.float32
    ).astype(jnp.bfloat16)
    zmat = factor.reshape(comp_here, rows_max, lines, 2 * width)
    wmat = jnp.concatenate([zmat[..., width:], -zmat[..., :width]], axis=-1)
    following = shifted(zmat[0], "mode", -1)
    partner = jnp.concatenate([zmat[1:], following[None]], axis=0)
    block = 128
    z_here = zmat[0]
    w_here = wmat[0]
    needed = (row_count[0] + block - 1) // block

    def block_step(step, buffer):
        z_rows = lax.dynamic_slice_in_dim(z_here, step * block, block, 0)
        w_rows = lax.dynamic_slice_in_dim(w_here, step * block, block, 0)
        part_re = (
            jnp.einsum("rfk,sfk->frs", z_rows, z_here, preferred_element_type=jnp.float32) / width
        )
        part_im = (
            jnp.einsum("rfk,sfk->frs", w_rows, z_here, preferred_element_type=jnp.float32) / width
        )
        value = jnp.stack([part_re, part_im], axis=1).astype(jnp.bfloat16)
        zero = jnp.zeros((), jnp.int32)
        return lax.dynamic_update_slice(
            buffer, value, (zero, zero, (step * block).astype(jnp.int32), zero)
        )

    empty = jnp.zeros((lines, 2, rows_max, rows_max), jnp.bfloat16)
    auto_blocks = [lax.fori_loop(0, needed, block_step, empty)]
    csd = jnp.stack(auto_blocks, axis=0)
    joint_re = (
        jnp.einsum("crfk,csfk->cfrs", zmat[:, :CROSS], partner, preferred_element_type=jnp.float32)
        / width
    )
    joint_im = (
        jnp.einsum("crfk,csfk->cfrs", wmat[:, :CROSS], partner, preferred_element_type=jnp.float32)
        / width
    )
    joint_csd = jnp.stack([joint_re, joint_im], axis=2).astype(jnp.bfloat16)
    return (csd, joint_csd)


def solution(mesh):
    return jax.shard_map(
        per_device,
        mesh=mesh,
        in_specs=(
            P(None, "mode"),
            P("mode"),
            P("mode"),
            P("freq"),
            P("mode", "freq", None, None),
            P(),
            P("mode"),
            P("mode", None, None),
        ),
        out_specs=(P("mode", "freq", None, None, None), P("mode", "freq", None, None, None)),
        check_vma=False,
    )
```

profile of v0, /device:TPU:16, one launch (start us, length us, event | category | flops | bytes accessed | tf_op | source)
XLA Modules:
  0.0 393.1 jit_solution(15512524188562069523)
XLA Ops:
  7.2 0.7 mul.124
  7.9 0.7 multiply_multiply_fusion.2
  8.6 0.7 fusion.22
  9.4 1.2 subtract_convert_fusion
  10.7 8.7 %convolution_bitcast_fusion = f32[6144,512]{0,1:T(8,128)} fusion(bf16[384,512]{0,1:T(8,128)(2,1)S(1)} %bitcast.55, bf16[6144,384]{1,0:T(8,128)(2,1)} %param.10), kind=kOutput, calls=%fused_computation.13 | convolution fusion | flops 2415919104 | bytes 17694720 | tf_op jit(solution)/shard_map/dot_general | solution.py:37
  19.4 12.6 %copy.34 = f32[6144,512]{1,0:T(8,128)} copy(f32[6144,512]{0,1:T(8,128)} %convolution_bitcast_fusion) | data formatting | bytes 25165824
  32.1 239.8 %reduce-scatter.4.cloned.1.call-done = f32[192,512]{1,0:T(8,128)} async-done(((f32[6144,512]{1,0:T(8,128)}), f32[192,512]{1,0:T(8,128)}) %reduce-scatter.4.cloned.1.call-update) | async-done | bytes 393232 | tf_op jit(solution)/shard_map/reduce_scatter | solution.py:36
  271.8 1.7 convert_element_type.23
  274.3 0.1 compare_and_fusion
  274.4 87.0 %all-gather.2.cloned.1.call-done = bf16[6144,512]{1,0:T(8,128)(2,1)} async-done(((bf16[192,512]{1,0:T(8,128)(2,1)}), bf16[6144,512]{1,0:T(8,128)(2,1)}) %all-gather.2.cloned.1.call-update) | async-done | bytes 6291472 | tf_op jit(solution)/shard_map/all_gather | solution.py:42
  361.4 4.4 %gather_fusion = bf16[96,512]{1,0:T(8,128)(2,1)S(1)} fusion(bf16[6144,512]{1,0:T(8,128)(2,1)} %all-gather.2.cloned.1.call-done, s32[1024]{0:T(1024)S(1)} %pad_clamp_fusion), kind=kCustom, calls=%fused_computation | custom fusion | bytes 196992 | tf_op jit(solution)/shard_map/jit(_take)/gather | solution.py:44
  365.8 0.3 convolution_convert_fusion
  366.2 0.1 reshape.262
  366.3 0.8 copy_bitcast_fusion
  367.1 0.4 fusion.28
  367.6 4.1 %collective-permute-start = (bf16[384,4,128]{2,0,1:T(8,128)(2,1)}, bf16[384,4,128]{2,0,1:T(8,128)(2,1)S(1)}, u32[]{:S(2)}, u32[]{:S(2)}) collective-permute-start(bf16[384,4,128]{2,0,1:T(8,128)(2,1)} %copy_bitcast_fusion), channel_id=1, source_target_pairs={{1,0},{2,1},{3,2},{4,3},{5,4},{6,5},{7,6},{8,7},{9,8},{10,9},{11,1... | collective-permute-start | bytes 1179656 | tf_op jit(solution)/shard_map/ppermute | solution.py:12
  371.7 0.2 maximum_bitcast_fusion
  371.9 1.6 broadcast_in_dim.21.clone
  373.5 11.0 %while.10 = (s32[]{:T(128)}, bf16[4,2,384,384]{3,2,1,0:T(8,128)(2,1)}, s32[]{:T(128)}, bf16[384,4,128]{2,0,1:T(8,128)(2,1)}, bf16[384,4,128]{2,0,1:T(8,128)(2,1)...) while((s32[]{:T(128)}, bf16[4,2,384,384]{3,2,1,0:T(8,128)(2,1)}, s32[]{:T(128)}, ...), condition=%wide.region_2.3_spmd, body=%wide.region_1.2_spmd.sunk | while | flops 101842944 | bytes 3408023 | solution.py:76
  373.5 1.3 fusion.46
  374.8 1.4 fusion.47
  376.2 1.0 copy_dynamic-update-slice_fusion.2
  377.2 1.3 fusion.46
  378.5 1.4 fusion.47
  379.9 1.0 copy_dynamic-update-slice_fusion.2
  380.9 1.3 fusion.46
  382.2 1.4 fusion.47
  383.5 1.0 copy_dynamic-update-slice_fusion.2
  384.6 0.3 fusion.10
  384.9 0.3 fusion.11
  385.2 0.1 pad_maximum_fusion.1
  385.3 1.0 copy.33
  (16 shorter events, 0.4 us)
Async XLA Ops:
  7.2 264.7 %reduce-scatter.4.cloned.1.call-start = ((), (), s32[]{:S(2)}) async-start(), calls=%async_computation.2 | async-start | bytes 12976128 | tf_op jit(solution)/shard_map/reduce_scatter | solution.py:36
  32.0 242.2 %copy-start.1 = (s32[32,96]{1,0:T(8,128)S(1)}, s32[32,96]{1,0:T(8,128)}, u32[]{:S(2)}) copy-start(s32[32,96]{1,0:T(8,128)} %param.15) | copy-start | bytes 36868
  32.0 333.9 %copy-start = (bf16[1,384,96]{1,2,0:T(8,128)(2,1)S(1)}, bf16[1,384,96]{1,2,0:T(8,128)(2,1)}, u32[]{:S(2)}) copy-start(bf16[1,384,96]{1,2,0:T(8,128)(2,1)} %param.17) | copy-start | bytes 221188
  32.0 329.4 %all-gather.2.cloned.1.call-start = ((), (), s32[]{:S(2)}) async-start(), calls=%async_computation.1 | async-start | bytes 6488064 | tf_op jit(solution)/shard_map/all_gather | solution.py:42
  367.6 17.0 %collective-permute-start = (bf16[384,4,128]{2,0,1:T(8,128)(2,1)}, bf16[384,4,128]{2,0,1:T(8,128)(2,1)S(1)}, u32[]{:S(2)}, u32[]{:S(2)}) collective-permute-start(bf16[384,4,128]{2,0,1:T(8,128)(2,1)} %copy_bitcast_fusion), channel_id=1, source_target_pairs={{1,0},{2,1},{3,2},{4,3},{5,4},{6,5},{7,6},{8,7},{9,8},{10,9},{11,1... | collective-permute-start | bytes 1179656 | tf_op jit(solution)/shard_map/ppermute | solution.py:12
Sparse Core Ops, SparseCore 0:
  32.1 239.6 reduce-scatter.3
  275.0 86.3 all-gather.1
where the time goes:
time: 394 us; the launch traced here: 393 us
  waiting for transfers between devices  327 us (83%)
  local copies, waits for them, and re-layouts  21 us (5%)
  matrix products  17.8 us (5%)
  between operations  14.8 us (4%)
  other arithmetic  8.52 us (2%)
  starting transfers between devices  4.16 us (1%)
    reduce_scatter x1, waiting for transfers between devices, per_device(): lax.psum_scatter(jnp.dot(mode_shapes, modal_resp, preferred_element_type=...  240 us
    all_gather x1, waiting for transfers between devices, per_device(): whole = lax.all_gather(band, 'mode', axis=0, tiled=True)  87 us
    unnamed x7, local copies, waits for them, and re-layouts  13.6 us
    dot_general x1, matrix products, per_device(): jnp.dot(mode_shapes, modal_resp, preferred_element_type=jnp.float32)  8.73 us
  transfers between devices with their start and end apart: 3, of which 2 were waited for; matrix products, arithmetic and copies ran while one was open for 3% of the time, Pallas kernels for 0%

commit v1 on v0

--- a/solution.py
+++ b/solution.py
@@ -1,9 +1,20 @@
+import functools
 import jax
 import jax.numpy as jnp
 from jax import lax
 from jax.sharding import PartitionSpec as P
 
 CROSS = 128
+
+
+def return_all_bands(xin, on_dim):
+    return jnp.concatenate(
+        jax.lax.all_to_all(jnp.stack([xin] * jax.lax.axis_size("mode"), axis=0), "mode", 0, 0),
+        on_dim,
+    )
+
+
+view_the_cubes = functools.partial(return_all_bands, on_dim=0)
 
 
 def shifted(value, axis, steps):
@@ -39,7 +50,7 @@
         scatter_dimension=0,
         tiled=True,
     ).astype(jnp.bfloat16)
-    whole = lax.all_gather(band, "mode", axis=0, tiled=True)
+    whole = view_the_cubes(band)
     index_rows = lax.dynamic_slice_in_dim(flat_attach, own_start, comp_here * att_len)
     picked = jnp.take(whole, index_rows, axis=0)
     picked = picked.reshape(comp_here, att_len, columns)

time: 394 us -> 453 us (1.15)
  waiting for transfers between devices: 327 us -> 374 us
  starting transfers between devices: 4.16 us -> 12 us
    all_to_all x0 -> x1, waiting for transfers between devices: none -> 134 us  [return_all_bands(): jax.lax.all_to_all(jnp.stack([xin] * jax.lax.axis_size('mode'), axis=0),...]
    all_gather x1 -> x0, waiting for transfers between devices: 87 us -> none  [per_device(): whole = lax.all_gather(band, 'mode', axis=0, tiled=True)]
    all_to_all x0 -> x1, starting transfers between devices: none -> 8.3 us  [return_all_bands(): jax.lax.all_to_all(jnp.stack([xin] * jax.lax.axis_size('mode'), axis=0),...]
where the time goes in v1:
time: 453 us; the launch traced here: 451 us
  waiting for transfers between devices  374 us (83%)
  local copies, waits for them, and re-layouts  24.4 us (5%)
  matrix products  17.8 us (4%)
  between operations  14.8 us (3%)
  starting transfers between devices  12 us (3%)
  other arithmetic  7.85 us (2%)
    reduce_scatter x1, waiting for transfers between devices, per_device(): lax.psum_scatter(jnp.dot(mode_shapes, modal_resp, preferred_element_type=...  240 us
    all_to_all x1, waiting for transfers between devices, return_all_bands(): jax.lax.all_to_all(jnp.stack([xin] * jax.lax.axis_size('mode'), axis=0),...  134 us
    unnamed x7, local copies, waits for them, and re-layouts  13.6 us
  transfers between devices with their start and end apart: 3, of which 2 were waited for; matrix products, arithmetic and copies ran while one was open for 3% of the time, Pallas kernels for 0%

profile of v1, /device:TPU:16, one launch (start us, length us, event | category | flops | bytes accessed | tf_op | source)
XLA Modules:
  0.0 451.1 jit_solution(3956189446963652829)
XLA Ops:
  7.2 0.7 mul.124
  7.9 0.7 multiply_multiply_fusion.2
  8.6 0.7 fusion.22
  9.4 1.2 subtract_convert_fusion
  10.7 8.7 %convolution_bitcast_fusion = f32[6144,512]{0,1:T(8,128)} fusion(bf16[384,512]{0,1:T(8,128)(2,1)S(1)} %bitcast.56, bf16[6144,384]{1,0:T(8,128)(2,1)} %param.10), kind=kOutput, calls=%fused_computation.13 | convolution fusion | flops 2415919104 | bytes 17694720 | tf_op jit(solution)/shard_map/dot_general | solution.py:48
  19.4 12.6 %copy.34 = f32[6144,512]{1,0:T(8,128)} copy(f32[6144,512]{0,1:T(8,128)} %convolution_bitcast_fusion) | data formatting | bytes 25165824
  32.0 239.8 %reduce-scatter.4.cloned.1.call-done = f32[192,512]{1,0:T(8,128)} async-done(((f32[6144,512]{1,0:T(8,128)}), f32[192,512]{1,0:T(8,128)}) %reduce-scatter.4.cloned.1.call-update) | async-done | bytes 393232 | tf_op jit(solution)/shard_map/reduce_scatter | solution.py:47
  271.8 1.0 convert_element_type.23
  272.9 3.4 stack.23
  276.2 8.3 %all-to-all-start = ((bf16[32,192,512]{2,1,0:T(8,128)(2,1)}), bf16[32,192,512]{2,1,0:T(8,128)(2,1)}, u32[]{:S(2)}, u32[]{:S(2)}) async-start(bf16[32,192,512]{2,1,0:T(8,128)(2,1)} %stack.23), calls=%async_computation | async-start | bytes 12582912 | tf_op jit(solution)/shard_map/all_to_all | solution.py:12
  285.4 134.4 %all-to-all-done = bf16[32,192,512]{2,1,0:T(8,128)(2,1)} async-done(((bf16[32,192,512]{2,1,0:T(8,128)(2,1)}), bf16[32,192,512]{2,1,0:T(8,128)(2,1)}, u32[]{:S(2)}, u32[]{:S(2)}) %all-to-all-start) | async-done | bytes 6291488 | tf_op jit(solution)/shard_map/all_to_all | solution.py:12
  419.8 4.4 gather_fusion
  424.2 0.3 convolution_convert_fusion
  424.5 0.1 reshape.268
  424.6 0.8 copy_bitcast_fusion
  425.4 0.4 fusion.28
  425.9 3.7 collective-permute-start
  429.6 0.2 maximum_bitcast_fusion
  429.9 1.6 broadcast_in_dim.21.clone
  431.5 11.0 %while.10 = (s32[]{:T(128)}, bf16[4,2,384,384]{3,2,1,0:T(8,128)(2,1)}, s32[]{:T(128)}, bf16[384,4,128]{2,0,1:T(8,128)(2,1)}, bf16[384,4,128]{2,0,1:T(8,128)(2,1)...) while((s32[]{:T(128)}, bf16[4,2,384,384]{3,2,1,0:T(8,128)(2,1)}, s32[]{:T(128)}, ...), condition=%wide.region_2.3_spmd, body=%wide.region_1.2_spmd.sunk | while | flops 101842944 | bytes 3408023 | solution.py:87
  431.5 1.3 fusion.46
  432.8 1.4 fusion.47
  434.2 1.0 copy_dynamic-update-slice_fusion.2
  435.1 1.3 fusion.46
  436.4 1.4 fusion.47
  437.8 1.0 copy_dynamic-update-slice_fusion.2
  438.8 1.3 fusion.46
  440.1 1.4 fusion.47
  441.5 1.0 copy_dynamic-update-slice_fusion.2
  442.5 0.4 fusion.10
  442.9 0.3 fusion.11
  443.3 1.0 copy.33
  (16 shorter events, 0.5 us)
Async XLA Ops:
  7.2 264.7 %reduce-scatter.4.cloned.1.call-start = ((), (), s32[]{:S(2)}) async-start(), calls=%async_computation.2 | async-start | bytes 12976128 | tf_op jit(solution)/shard_map/reduce_scatter | solution.py:47
  276.2 9.0 %copy-start.1 = (s32[32,96]{1,0:T(8,128)S(1)}, s32[32,96]{1,0:T(8,128)}, u32[]{:S(2)}) copy-start(s32[32,96]{1,0:T(8,128)} %param.15) | copy-start | bytes 36868
  276.2 147.9 %copy-start = (bf16[1,384,96]{1,2,0:T(8,128)(2,1)S(1)}, bf16[1,384,96]{1,2,0:T(8,128)(2,1)}, u32[]{:S(2)}) copy-start(bf16[1,384,96]{1,2,0:T(8,128)(2,1)} %param.17) | copy-start | bytes 221188
  276.2 143.6 %all-to-all-start = ((bf16[32,192,512]{2,1,0:T(8,128)(2,1)}), bf16[32,192,512]{2,1,0:T(8,128)(2,1)}, u32[]{:S(2)}, u32[]{:S(2)}) async-start(bf16[32,192,512]{2,1,0:T(8,128)(2,1)} %stack.23), calls=%async_computation | async-start | bytes 12582912 | tf_op jit(solution)/shard_map/all_to_all | solution.py:12
  425.9 16.6 %collective-permute-start = (bf16[384,4,128]{2,0,1:T(8,128)(2,1)}, bf16[384,4,128]{2,0,1:T(8,128)(2,1)S(1)}, u32[]{:S(2)}, u32[]{:S(2)}) collective-permute-start(bf16[384,4,128]{2,0,1:T(8,128)(2,1)} %copy_bitcast_fusion), channel_id=1, source_target_pairs={{1,0},{2,1},{3,2},{4,3},{5,4},{6,5},{7,6},{8,7},{9,8},{10,9},{11,1... | collective-permute-start | bytes 1179656 | tf_op jit(solution)/shard_map/ppermute | solution.py:23
Sparse Core Ops, SparseCore 0:
  32.1 239.6 reduce-scatter.3
